TPU v7x, 32 devices: a whole 2x2x4 slice. The times are simulated.
32 devices in a mesh: section: 4 (over z), dp: 8 (over y, x, core).
Axes of the slice: x: 2, y: 2, z: 4, core: 2. Of those that a mesh axis runs over, the one named last changes fastest.
Arguments:
- acts: bfloat16 [4, 3072, 8192], P('section', 'dp'), may hold values from -6 to 6
- input_grads: bfloat16 [4, 3072, 5120], P('section', 'dp'), may hold values from -6 to 6
- head_grads: bfloat16 [3072, 5120], P('dp'), may hold values from -6 to 6
- weight_grad: bfloat16 [4, 5120, 8192], P('section', None, 'dp'), may hold values from -6 to 6
- sweeps: int32 [4, 52], P('section'), may hold values from 1 to 4
Outputs:
- update: bfloat16 [4, 5120, 8192], P('section', None, 'dp')
Inputs may be any that keep to these rules, and one draw needn't show every extreme that they name: sweeps[s, k] is the number of Newton-Schulz iterations of block k of layer s; every value from 1 to 4 occurs.
All inputs are finite; a program needn't handle non-finite values. Where the computation divides by a largest or mean magnitude, that divisor is 1e-20 or more.
Results may differ from a plain program's by a relative error of at most 0.0067.
Values may be sent and summed in bfloat16 or wider, within the bound.
No kernel may reach another device: no remote copies, remote signals or barrier semaphores. Data moves between devices by JAX's collectives and lax.ppermute only.
A program may use at most 128 MiB of HBM per device.

v0:
```python
import functools

import jax
import jax.numpy as jnp
from jax import lax
from jax.experimental import pallas as pl
from jax.experimental.pallas import tpu as pltpu
from jax.sharding import PartitionSpec as P


BLOCK = 256
HALF = BLOCK // 2
PAD = 16
NS_MAX = 4

damping = 0.05


def masks():
    row = lax.broadcasted_iota(jnp.int32, (HALF, HALF), 0)
    col = lax.broadcasted_iota(jnp.int32, (HALF, HALF), 1)
    return row, col


def pack_block(full, row, col):
    upper = full[:HALF, HALF:]
    second = full[HALF:, HALF:]
    mixed = jnp.where(row >= col, full[:HALF, :HALF], second)
    line = jnp.sum(jnp.where(row == col, second, 0.0), axis=0, keepdims=True)
    return upper, mixed, line


def unpack_block(upper, mixed, line, row, col):
    turned = mixed.T
    first = jnp.where(row >= col, mixed, turned)
    second = jnp.where(row < col, mixed, jnp.where(row > col, turned, line))
    top = jnp.concatenate([first, upper], axis=1)
    bottom = jnp.concatenate([upper.T, second], axis=1)
    return jnp.concatenate([top, bottom], axis=0)


def store_unit(out, index, blocks, row, col):
    count = len(blocks)
    lines = jnp.zeros((PAD, HALF), jnp.float32)
    place = lax.broadcasted_iota(jnp.int32, (PAD, HALF), 0)
    for j, full in enumerate(blocks):
        upper, mixed, line = pack_block(full, row, col)
        out[index + (pl.ds(j * BLOCK, HALF),)] = upper.astype(out.dtype)
        out[index + (pl.ds(j * BLOCK + HALF, HALF),)] = mixed.astype(out.dtype)
        lines = jnp.where(place == j, line, lines)
    out[index + (pl.ds(count * BLOCK, PAD),)] = lines.astype(out.dtype)


def gram(x):
    return lax.dot_general(x, x, (((0,), (0,)), ((), ())), preferred_element_type=jnp.float32)


def shares(blocks, dp_count):
    share, rest = blocks // dp_count, blocks % dp_count
    return share, -(-rest // (dp_count // 2))


def owned_block(owner, slot, blocks, dp_count):
    share, _ = shares(blocks, dp_count)
    if slot < share:
        return owner * share + slot
    chips = dp_count // 2
    return jnp.minimum(share * dp_count + owner // 2 + chips * (slot - share), blocks - 1)


def factor_kernel(blocks, dp_count, parities, choices, keep, *refs):
    slots = sum(shares(blocks, dp_count))
    me = lax.axis_index("dp")
    sources = refs[: max(choices, 1)]
    if choices:
        sems, columns = refs[-1], refs[-2]
        outs = refs[-2 - len(parities) : -2]
        chunks = sems.shape[0]
        rows = columns.shape[0] // chunks

        def fetch(source, i):
            place = pl.ds(i * rows, rows)
            view = source.at[0, place] if len(source.shape) == 3 else source.at[place]
            return pltpu.make_async_copy(view, columns.at[place], sems.at[i])

        def fetch_all(source):
            for i in range(chunks):
                fetch(source, i).start()

        if choices == 1:
            fetch_all(sources[0])
        else:
            first = lax.axis_index("section") == 0
            pl.when(first)(lambda: fetch_all(sources[1]))
            pl.when(jnp.logical_not(first))(lambda: fetch_all(sources[0]))
        for i in range(chunks):
            fetch(sources[0], i).wait()
    else:
        columns, outs = refs[0], refs[-len(parities) :]
    row, col = masks()
    for parity, out in zip(parities, outs):
        for step in range(dp_count // 2):
            grams = []
            for slot in range(slots):
                block = owned_block(me ^ (2 * step + parity), slot, blocks, dp_count)
                place = pl.ds(pl.multiple_of(block * BLOCK, BLOCK), BLOCK)
                grams.append(gram(columns[:, place]))
            store_unit(out, (step,), grams, row, col)


def partial_factors(sources, dp_count, parities, keep=False, loaded=False, after=()):
    tokens, width = sources[0].shape[-2:]
    blocks = width // BLOCK
    unit = sum(shares(blocks, dp_count)) * BLOCK + PAD
    outs = [pltpu.VMEM((dp_count // 2, unit, HALF), jnp.bfloat16)] * len(parities)
    columns = pltpu.VMEM((tokens, width), jnp.bfloat16)
    vmem = pl.BlockSpec(memory_space=pltpu.VMEM)
    scratch = [] if loaded else [pltpu.SemaphoreType.DMA((4,))]
    if keep:
        outs.append(columns)
    elif not loaded:
        scratch.insert(0, columns)
    space = pltpu.VMEM if loaded else pltpu.HBM
    specs = [pl.BlockSpec(memory_space=space)] * len(sources)
    return pl.pallas_call(
        functools.partial(
            factor_kernel, blocks, dp_count, parities, 0 if loaded else len(sources), keep
        ),
        out_shape=tuple(outs),
        in_specs=specs + [pl.BlockSpec(memory_space=pl.ANY)] * len(after),
        out_specs=tuple([vmem] * len(outs)),
        scratch_shapes=scratch,
        compiler_params=pltpu.CompilerParams(vmem_limit_bytes=20 << 20),
        cost_estimate=pl.CostEstimate(
            flops=len(parities) * tokens * width * BLOCK,
            bytes_accessed=tokens * width * 3,
            transcendentals=0,
        ),
    )(*[pltpu.with_memory_space_constraint(source, space) for source in sources], *after)


def split(a):
    high = a.astype(jnp.bfloat16)
    return high, (a - high.astype(jnp.float32)).astype(jnp.bfloat16)


def product(a, b):
    def dot(x, y):
        return jnp.dot(x, y, preferred_element_type=jnp.float32)

    return dot(a[0], b[0]) + (dot(a[0], b[1]) + dot(a[1], b[0]))


def newton(matrices, counts):
    row = lax.broadcasted_iota(jnp.int32, (BLOCK, BLOCK), 0)
    col = lax.broadcasted_iota(jnp.int32, (BLOCK, BLOCK), 1)
    eye = (row == col).astype(jnp.float32)
    rest, found = [], []
    for matrix in matrices:
        scale = 1.0 / jnp.max(jnp.sum(jnp.abs(matrix), axis=0, keepdims=True), axis=1, keepdims=True)
        left = eye - scale * matrix
        rest.append(left)
        found.append(scale * (eye + left))
    for turn in range(1, NS_MAX):
        parts = [split(left) for left in rest]
        rest = [product(part, part) for part in parts]
        squares = [split(left) for left in rest]
        step = [product(split(x), square) for x, square in zip(found, squares)]
        found = [jnp.where(turn < count, x + more, x) for x, more, count in zip(found, step, counts)]
    return found


def summed_factors(refs, slots, token_total, row, col):
    parts = []
    for ref in refs:
        parts.append(ref[0] if len(ref.shape) == 3 else ref[...])
    total = sum(part.astype(jnp.float32) for part in parts) * (1.0 / token_total)
    wide_row = lax.broadcasted_iota(jnp.int32, (BLOCK, BLOCK), 0)
    wide_col = lax.broadcasted_iota(jnp.int32, (BLOCK, BLOCK), 1)
    shift = jnp.where(wide_row == wide_col, damping, 0.0)
    blocks = []
    for j in range(slots):
        upper = total[j * BLOCK : j * BLOCK + HALF]
        mixed = total[j * BLOCK + HALF : (j + 1) * BLOCK]
        line = total[slots * BLOCK + j : slots * BLOCK + j + 1]
        blocks.append(unpack_block(upper, mixed, line, row, col) + shift)
    return blocks


def gather_rows(blocks, dp_count):
    share, extra = shares(blocks, dp_count)
    return share * BLOCK + extra * HALF + PAD


def invert_kernel(hidden_blocks, blocks, dp_count, token_total, sweeps, *refs):
    out = refs[-1]
    row, col = masks()
    share, extra = shares(blocks, dp_count)
    slots = share + extra
    me = lax.axis_index("dp")
    factors = summed_factors(refs[:-1], slots, token_total, row, col)
    counts = [
        sweeps[0, hidden_blocks + owned_block(me, j, blocks, dp_count)] for j in range(slots)
    ]
    lines = jnp.zeros((PAD, HALF), jnp.float32)
    place = lax.broadcasted_iota(jnp.int32, (PAD, HALF), 0)
    even = me % 2 == 0
    for j, full in enumerate(newton(factors, counts)):
        upper, mixed, line = pack_block(full, row, col)
        lines = jnp.where(place == j, line, lines)
        if j < share:
            out[pl.ds(j * BLOCK, HALF)] = upper.astype(out.dtype)
            out[pl.ds(j * BLOCK + HALF, HALF)] = mixed.astype(out.dtype)
        else:
            own = jnp.where(even, upper, mixed)
            out[pl.ds(share * BLOCK + (j - share) * HALF, HALF)] = own.astype(out.dtype)
    out[pl.ds(share * BLOCK + extra * HALF, PAD)] = lines.astype(out.dtype)


def unit_specs(own, others):
    unit = own.shape[1]
    front = pl.BlockSpec((1, unit, HALF), lambda g, *_: (0, 0, 0))
    whole = pl.BlockSpec((unit, HALF), lambda g, *_: (0, 0))
    return [front, front] + [whole] * len(others)


def invert_units(sweeps, own, first, others, hidden_blocks, blocks, dp_count, token_total):
    unit = gather_rows(blocks, dp_count)
    slots = sum(shares(blocks, dp_count))
    return pl.pallas_call(
        functools.partial(invert_kernel, hidden_blocks, blocks, dp_count, token_total),
        out_shape=jax.ShapeDtypeStruct((unit, HALF), jnp.bfloat16),
        grid_spec=pltpu.PrefetchScalarGridSpec(
            num_scalar_prefetch=1,
            grid=(1,),
            in_specs=unit_specs(own, others),
            out_specs=pl.BlockSpec((unit, HALF), lambda g, *_: (0, 0)),
        ),
        compiler_params=pltpu.CompilerParams(vmem_limit_bytes=16 << 20),
        cost_estimate=pl.CostEstimate(
            flops=36 * slots * BLOCK**3, bytes_accessed=12 * slots * BLOCK * BLOCK, transcendentals=0
        ),
    )(sweeps, own, first, *others)


def half_kernel(slots, token_total, sweeps, *refs):
    weights, out = refs[-2:]
    row, col = masks()
    me = lax.axis_index("dp")
    factors = summed_factors(refs[:-2], slots, token_total, row, col)
    found = newton(factors, [sweeps[0, me * slots + j] for j in range(slots)])
    for j in range(slots):
        columns = slice(j * BLOCK, (j + 1) * BLOCK)
        value = jnp.dot(
            weights[0, :, columns],
            found[j].astype(jnp.bfloat16),
            preferred_element_type=jnp.float32,
        )
        out[:, columns] = value.astype(jnp.bfloat16)


def half_update(sweeps, own, first, others, token_total, weight_grad):
    _, depth, columns = weight_grad.shape
    slots = columns // BLOCK
    specs = unit_specs(own, others) + [pl.BlockSpec(memory_space=pltpu.VMEM)]
    return pl.pallas_call(
        functools.partial(half_kernel, slots, token_total),
        out_shape=pltpu.VMEM((depth, columns), jnp.bfloat16),
        grid_spec=pltpu.PrefetchScalarGridSpec(
            num_scalar_prefetch=1,
            grid=(1,),
            in_specs=specs,
            out_specs=pl.BlockSpec(memory_space=pltpu.VMEM),
        ),
        compiler_params=pltpu.CompilerParams(vmem_limit_bytes=30 << 20),
        cost_estimate=pl.CostEstimate(
            flops=36 * slots * BLOCK**3 + 2 * depth * columns * BLOCK,
            bytes_accessed=2 * depth * columns,
            transcendentals=0,
        ),
    )(sweeps, own, first, *others, pltpu.with_memory_space_constraint(weight_grad, pltpu.VMEM))


def update_kernel(blocks, dp_count, *refs):
    half, out, staged, sems = refs[-4:]
    units = refs[:-4]
    share, extra = shares(blocks, dp_count)
    me = lax.axis_index("dp")
    row, col = masks()
    even = me % 2 == 0

    def copy(step, block):
        place = pl.ds(pl.multiple_of(block * BLOCK, BLOCK), BLOCK)
        return pltpu.make_async_copy(staged.at[step], out.at[0, place], sems.at[step])

    def tile(unit, start, rows=HALF):
        return unit[start : start + rows, :].astype(jnp.float32)

    def one(step, r, slot):
        near, far = units[r // 2], units[(dp_count + r) // 2]
        owner = me ^ r
        if slot >= 2 * share:
            slot -= share
            start = share * BLOCK + (slot - share) * HALF
            own, other = tile(near, start), tile(far, start)
            upper, mixed = jnp.where(even, own, other), jnp.where(even, other, own)
        else:
            if slot >= share:
                near, owner, slot = far, owner ^ 1, slot - share
            upper, mixed = tile(near, slot * BLOCK), tile(near, slot * BLOCK + HALF)
        block = owned_block(owner, slot, blocks, dp_count)
        line = tile(near, share * BLOCK + extra * HALF, PAD)[slot : slot + 1]
        full = unpack_block(upper, mixed, line, row, col).astype(jnp.bfloat16)
        place = pl.ds(pl.multiple_of(block * BLOCK, BLOCK), BLOCK)
        value = jnp.dot(full, half[place, :], preferred_element_type=jnp.float32)
        staged[step] = value.astype(jnp.bfloat16)
        copy(step, block).start()

    def guarded(r, slot, run):
        chips, rest = dp_count // 2, blocks % dp_count
        if slot < 2 * share or rest == chips * extra:
            run()
        else:
            pl.when((me ^ r) // 2 + chips * (slot - 2 * share) < rest)(run)

    steps = [(r, slot) for r in range(0, dp_count, 2) for slot in range(2 * share + extra)]
    for step, (r, slot) in enumerate(steps):
        guarded(r, slot, functools.partial(one, step, r, slot))
    for step, (r, slot) in enumerate(steps):
        guarded(r, slot, lambda: copy(step, 0).wait())


def final_update(units, half, dp_count):
    depth, columns = half.shape
    blocks = depth // BLOCK
    share, extra = shares(blocks, dp_count)
    steps = dp_count // 2 * (2 * share + extra)
    return pl.pallas_call(
        functools.partial(update_kernel, blocks, dp_count),
        out_shape=jax.ShapeDtypeStruct((1, depth, columns), jnp.bfloat16),
        in_specs=[pl.BlockSpec(memory_space=pltpu.VMEM)] * (len(units) + 1),
        out_specs=pl.BlockSpec(memory_space=pl.ANY),
        scratch_shapes=[
            pltpu.VMEM((steps, BLOCK, columns), jnp.bfloat16),
            pltpu.SemaphoreType.DMA((steps,)),
        ],
        compiler_params=pltpu.CompilerParams(vmem_limit_bytes=30 << 20),
        cost_estimate=pl.CostEstimate(
            flops=2 * depth * columns * BLOCK, bytes_accessed=2 * depth * columns, transcendentals=0
        ),
    )(*units, pltpu.with_memory_space_constraint(half, pltpu.VMEM))


def swap(value, distance):
    count = lax.axis_size("dp")
    return lax.ppermute(value, "dp", [(i, i ^ distance) for i in range(count)])


def spread(keep, first, dp_count):
    others = []
    for r in range(2, dp_count, 2):
        value = keep[r // 2].astype(jnp.float32) + first[r // 2].astype(jnp.float32)
        others.append(swap(value.astype(jnp.bfloat16), r))
    return others


def whole(acts, input_grads, head_grads, weight_grad, sweeps):
    dp_count = lax.axis_size("dp")
    section_count = lax.axis_size("section")
    tokens = acts.shape[1] * dp_count
    hidden_blocks = acts.shape[2] // BLOCK
    model_blocks = input_grads.shape[2] // BLOCK
    back = [((s + 1) % section_count, s) for s in range(section_count)]
    ahead = [(s, (s + 1) % section_count) for s in range(section_count)]

    send_g, grads = partial_factors([input_grads, head_grads], dp_count, (1,), keep=True)
    first_g = swap(send_g, 1)
    (keep_g,) = partial_factors([grads], dp_count, (0,), loaded=True)
    their_sweeps = lax.ppermute(sweeps, "section", ahead)
    send_a, keep_a = partial_factors([acts], dp_count, (1, 0), after=(keep_g,))
    others_g = spread(keep_g, first_g, dp_count)
    first_a = swap(send_a, 1)
    unit = invert_units(
        their_sweeps, keep_g, first_g, others_g, hidden_blocks, model_blocks, dp_count, tokens
    )
    others_a = spread(keep_a, first_a, dp_count)
    unit = lax.ppermute(unit, "section", back)
    even = [unit] + [swap(unit, r) for r in range(2, dp_count, 2)]
    half = half_update(sweeps, keep_a, first_a, others_a, tokens, weight_grad)
    odd = [swap(value, 1) for value in even]
    return final_update(even + odd, half, dp_count)


def solution(mesh):
    return jax.shard_map(
        whole,
        mesh=mesh,
        in_specs=(
            P("section", "dp", None),
            P("section", "dp", None),
            P("dp", None),
            P("section", None, "dp"),
            P("section", None),
        ),
        out_specs=P("section", None, "dp"),
        check_vma=False,
    )
```

profile of v0, /device:TPU:0, one launch (start us, length us, event | category | flops | bytes accessed | tf_op | source)
XLA Modules:
  0.0 62.9 jit_solution(3004070875371243813)
XLA Ops:
  0.0 3.2 %shard_map.55 = (bf16[4,784,128]{2,1,0:T(8,128)(2,1)S(1)}, bf16[384,5120]{1,0:T(8,128)(2,1)S(1)}) custom-call(bf16[1,384,5120]{2,1,0:T(8,128)(2,1)} %refs_0_.2, bf16[384,5120]{1,0:T(8,128)(2,1)} %refs_1_.1), custom_call_target="tpu_custom_call" | custom-call | flops 503316480 | bytes 5898240 | tf_op jit(solution)/shard_map/pallas_call | solution.py:125
  3.2 1.1 %shard_map.56.refs_0_.refs_1_ = bf16[4,784,128]{2,1,0:T(8,128)(2,1)S(1)} custom-call(bf16[384,5120]{1,0:T(8,128)(2,1)S(1)} %get-tuple-element.9.refs_0_), custom_call_target="tpu_custom_call" | custom-call | flops 503316480 | bytes 5898240 | tf_op jit(solution)/shard_map/pallas_call | solution.py:125
  4.3 5.6 %shard_map.58 = (bf16[4,1040,128]{2,1,0:T(8,128)(2,1)S(1)}, bf16[4,1040,128]{2,1,0:T(8,128)(2,1)S(1)}) custom-call(bf16[1,384,8192]{2,1,0:T(8,128)(2,1)} %refs_0_.3, bf16[4,784,128]{2,1,0:T(8,128)(2,1)S(1)} %shard_map.56.refs_0_.refs_1_), custom_call_target="tpu_custom_call" | custom-call | flops 1610612736 | bytes 9437184 | tf_op jit(solution)/shard_map/pallas_call | solution.py:125
  9.9 0.6 collective-permute-start.13
  10.5 3.0 %collective-permute-start = (s32[1,52]{1,0:T(1,128)S(1)}, s32[1,52]{1,0:T(1,128)S(1)}, u32[]{:S(2)}, u32[]{:S(2)}) collective-permute-start(s32[1,52]{1,0:T(1,128)S(1)} %copy-done), channel_id=1, source_target_pairs={{0,8},{8,16},{16,24},{24,0},{1,9},{9,17},{17,25},{25,1},{2,10},{10... | collective-permute-start | bytes 632 | tf_op jit(solution)/shard_map/ppermute | solution.py:379
  14.1 3.9 %collective-permute-start.4 = (bf16[784,128]{1,0:T(8,128)(2,1)S(1)}, bf16[784,128]{1,0:T(8,128)(2,1)S(1)}, u32[]{:S(2)}, u32[]{:S(2)}) collective-permute-start(bf16[784,128]{1,0:T(8,128)(2,1)S(1)} %get-tuple-element.16), channel_id=1, source_target_pairs={{0,6},{1,7},{2,4},{3,5},{4,2},{5,3},{6,0},{7,1},{8,14},{9,15},{10,... | collective-permute-start | bytes 602120 | tf_op jit(solution)/shard_map/ppermute | solution.py:356
  18.8 2.9 %collective-permute-start.16 = (bf16[1040,128]{1,0:T(8,128)(2,1)S(1)}, bf16[1040,128]{1,0:T(8,128)(2,1)S(1)}, u32[]{:S(2)}, u32[]{:S(2)}) collective-permute-start(bf16[1040,128]{1,0:T(8,128)(2,1)S(1)} %get-tuple-element.13), channel_id=1, source_target_pairs={{0,6},{1,7},{2,4},{3,5},{4,2},{5,3},{6,0},{7,1},{8,14},{9,15},{10,... | collective-permute-start | bytes 798728 | tf_op jit(solution)/shard_map/ppermute | solution.py:356
  21.7 2.1 %collective-permute-done.4.refs_4_ = bf16[784,128]{1,0:T(8,128)(2,1)S(1)} collective-permute-done((bf16[784,128]{1,0:T(8,128)(2,1)S(1)}, bf16[784,128]{1,0:T(8,128)(2,1)S(1)}, u32[]{:S(2)}, u32[]{:S(2)}) %collective-permute-start.4) | collective-permute-done | bytes 200736 | tf_op jit(solution)/shard_map/ppermute | solution.py:356
  23.8 4.2 %collective-permute-done.3.refs_3_ = bf16[784,128]{1,0:T(8,128)(2,1)S(1)} collective-permute-done((bf16[784,128]{1,0:T(8,128)(2,1)S(1)}, bf16[784,128]{1,0:T(8,128)(2,1)S(1)}, u32[]{:S(2)}, u32[]{:S(2)}) %collective-permute-start.3) | collective-permute-done | bytes 200736 | tf_op jit(solution)/shard_map/ppermute | solution.py:356
  28.0 0.6 collective-permute-done.2.refs_2_
  28.6 3.1 %shard_map.57 = bf16[656,128]{1,0:T(8,128)(2,1)S(1)} custom-call(s32[1,52]{1,0:T(1,128)S(1)} %collective-permute-done.sweeps, bf16[4,784,128]{2,1,0:T(8,128)(2,1)S(1)} %shard_map.56.refs_0_.refs_1_, bf16[4,784,128]{2,1,0:T(8,128)(2,1)S(1)} %collective-permute-done.1.refs_1_, bf16[784,128]{1,0:T(8,128)(2,1)S(1)} %collective-permute-done.2.refs_2_, ...), custom_call_target="tpu_custom_call" | custom-call | flops 1811939328 | bytes 2359296 | tf_op jit(solution)/shard_map/pallas_call | solution.py:230
  31.7 3.8 %collective-permute-start.5 = (bf16[656,128]{1,0:T(8,128)(2,1)S(1)}, bf16[656,128]{1,0:T(8,128)(2,1)S(1)}, u32[]{:S(2)}, u32[]{:S(2)}) collective-permute-start(bf16[656,128]{1,0:T(8,128)(2,1)S(1)} %shard_map.57), channel_id=1, source_target_pairs={{8,0},{16,8},{24,16},{0,24},{9,1},{17,9},{25,17},{1,25},{10,2},{18... | collective-permute-start | bytes 503816 | tf_op jit(solution)/shard_map/ppermute | solution.py:387
  35.6 1.4 %collective-permute-start.15 = (bf16[1040,128]{1,0:T(8,128)(2,1)S(1)}, bf16[1040,128]{1,0:T(8,128)(2,1)S(1)}, u32[]{:S(2)}, u32[]{:S(2)}) collective-permute-start(bf16[1040,128]{1,0:T(8,128)(2,1)S(1)} %get-tuple-element.14), channel_id=1, source_target_pairs={{0,4},{1,5},{2,6},{3,7},{4,0},{5,1},{6,2},{7,3},{8,12},{9,13},{10,... | collective-permute-start | bytes 798728 | tf_op jit(solution)/shard_map/ppermute | solution.py:356
  37.0 0.6 collective-permute-start.14
  37.6 1.5 %collective-permute-done.5.refs_0_ = bf16[656,128]{1,0:T(8,128)(2,1)S(1)} collective-permute-done((bf16[656,128]{1,0:T(8,128)(2,1)S(1)}, bf16[656,128]{1,0:T(8,128)(2,1)S(1)}, u32[]{:S(2)}, u32[]{:S(2)}) %collective-permute-start.5) | collective-permute-done | bytes 167968 | tf_op jit(solution)/shard_map/ppermute | solution.py:387
  39.1 0.8 %collective-permute-start.8 = (bf16[656,128]{1,0:T(8,128)(2,1)S(1)}, bf16[656,128]{1,0:T(8,128)(2,1)S(1)}, u32[]{:S(2)}, u32[]{:S(2)}) collective-permute-start(bf16[656,128]{1,0:T(8,128)(2,1)S(1)} %collective-permute-done.5.refs_0_), channel_id=1, source_target_pairs={{0,6},{1,7},{2,4},{3,5},{4,2},{5,3},{6,0},{7,1},{8,14},{9,15},{10,... | collective-permute-start | bytes 503816 | tf_op jit(solution)/shard_map/ppermute | solution.py:356
  39.9 2.1 %collective-permute-start.7 = (bf16[656,128]{1,0:T(8,128)(2,1)S(1)}, bf16[656,128]{1,0:T(8,128)(2,1)S(1)}, u32[]{:S(2)}, u32[]{:S(2)}) collective-permute-start(bf16[656,128]{1,0:T(8,128)(2,1)S(1)} %collective-permute-done.5.refs_0_), channel_id=1, source_target_pairs={{0,4},{1,5},{2,6},{3,7},{4,0},{5,1},{6,2},{7,3},{8,12},{9,13},{10,... | collective-permute-start | bytes 503816 | tf_op jit(solution)/shard_map/ppermute | solution.py:356
  42.0 0.5 collective-permute-start.6
  42.6 4.4 %collective-permute-done.15.refs_3_ = bf16[1040,128]{1,0:T(8,128)(2,1)S(1)} collective-permute-done((bf16[1040,128]{1,0:T(8,128)(2,1)S(1)}, bf16[1040,128]{1,0:T(8,128)(2,1)S(1)}, u32[]{:S(2)}, u32[]{:S(2)}) %collective-permute-start.15) | collective-permute-done | bytes 266272 | tf_op jit(solution)/shard_map/ppermute | solution.py:356
  47.0 2.9 %collective-permute-done.8.refs_3_ = bf16[656,128]{1,0:T(8,128)(2,1)S(1)} collective-permute-done((bf16[656,128]{1,0:T(8,128)(2,1)S(1)}, bf16[656,128]{1,0:T(8,128)(2,1)S(1)}, u32[]{:S(2)}, u32[]{:S(2)}) %collective-permute-start.8) | collective-permute-done | bytes 167968 | tf_op jit(solution)/shard_map/ppermute | solution.py:356
  49.9 0.7 %collective-permute-done.7.refs_2_ = bf16[656,128]{1,0:T(8,128)(2,1)S(1)} collective-permute-done((bf16[656,128]{1,0:T(8,128)(2,1)S(1)}, bf16[656,128]{1,0:T(8,128)(2,1)S(1)}, u32[]{:S(2)}, u32[]{:S(2)}) %collective-permute-start.7) | collective-permute-done | bytes 167968 | tf_op jit(solution)/shard_map/ppermute | solution.py:356
  50.6 1.2 %collective-permute-done.6.refs_1_ = bf16[656,128]{1,0:T(8,128)(2,1)S(1)} collective-permute-done((bf16[656,128]{1,0:T(8,128)(2,1)S(1)}, bf16[656,128]{1,0:T(8,128)(2,1)S(1)}, u32[]{:S(2)}, u32[]{:S(2)}) %collective-permute-start.6) | collective-permute-done | bytes 167968 | tf_op jit(solution)/shard_map/ppermute | solution.py:356
  51.9 6.4 %shard_map.59.refs_8_ = bf16[5120,1024]{1,0:T(8,128)(2,1)S(1)} custom-call(s32[1,52]{1,0:T(1,128)S(1)} %copy-done, bf16[4,1040,128]{2,1,0:T(8,128)(2,1)S(1)} %get-tuple-element.11.refs_0_, bf16[4,1040,128]{2,1,0:T(8,128)(2,1)S(1)} %collective-permute-done.13.refs_1_, bf16[1040,128]{1,0:T(8,128)(2,1)S(1)} %collective-permute-done.14.refs_2_, ...), custom_call_target="tpu_custom_call" | custom-call | flops 5100273664 | bytes 10485760 | tf_op jit(solution)/shard_map/pallas_call | solution.py:266
  58.3 4.4 %shard_map.60 = bf16[1,5120,1024]{2,1,0:T(8,128)(2,1)} custom-call(bf16[656,128]{1,0:T(8,128)(2,1)S(1)} %collective-permute-done.5.refs_0_, bf16[656,128]{1,0:T(8,128)(2,1)S(1)} %collective-permute-done.6.refs_1_, bf16[656,128]{1,0:T(8,128)(2,1)S(1)} %collective-permute-done.7.refs_2_, bf16[656,128]{1,0:T(8,128)(2,1)S(1)} %collective-permute-done.8.refs_3_, ...), custom_call_target="tpu_custom_call" | custom-call | flops 2684354560 | bytes 10485760 | tf_op jit(solution)/shard_map/pallas_call | solution.py:338
  (27 shorter events, 1.5 us)
Async XLA Ops:
  3.2 48.6 %slice-start = ((s8[10485760]{0:T(1024)(128)(4,1)}), s8[4194304]{0:T(1024)(128)(4,1)S(1)}, s32[]{:S(2)}) async-start(s8[10485760]{0:T(1024)(128)(4,1)} %bitcast.12), calls=%async_computation | async-start | bytes 8388608
  4.3 6.2 %copy-start = (s32[1,52]{1,0:T(1,128)S(1)}, s32[1,52]{1,0:T(1,128)}, u32[]{:S(2)}) copy-start(s32[1,52]{1,0:T(1,128)} %sweeps.1) | copy-start | bytes 628
  4.3 47.5 %slice-start.1 = ((s8[10485760]{0:T(1024)(128)(4,1)}), s8[4194304]{0:T(1024)(128)(4,1)S(1)}, s32[]{:S(2)}) async-start(s8[10485760]{0:T(1024)(128)(4,1)} %bitcast.12), calls=%async_computation.1 | async-start | bytes 8388608
  9.9 8.7 %collective-permute-start.13 = (bf16[4,1040,128]{2,1,0:T(8,128)(2,1)S(1)}, bf16[4,1040,128]{2,1,0:T(8,128)(2,1)S(1)}, u32[]{:S(2)}, u32[]{:S(2)}) collective-permute-start(bf16[4,1040,128]{2,1,0:T(8,128)(2,1)S(1)} %get-tuple-element.12), channel_id=1, source_target_pairs={{0,1},{1,0},{2,3},{3,2},{4,5},{5,4},{6,7},{7,6},{8,9},{9,8},{10,11... | collective-permute-start | bytes 3194888 | tf_op jit(solution)/shard_map/ppermute | solution.py:356
  10.4 3.5 %collective-permute-start.1 = (bf16[4,784,128]{2,1,0:T(8,128)(2,1)S(1)}, bf16[4,784,128]{2,1,0:T(8,128)(2,1)S(1)}, u32[]{:S(2)}, u32[]{:S(2)}) collective-permute-start(bf16[4,784,128]{2,1,0:T(8,128)(2,1)S(1)} %get-tuple-element.10), channel_id=1, source_target_pairs={{0,1},{1,0},{2,3},{3,2},{4,5},{5,4},{6,7},{7,6},{8,9},{9,8},{10,11... | collective-permute-start | bytes 2408456 | tf_op jit(solution)/shard_map/ppermute | solution.py:356
  10.5 11.2 %collective-permute-start = (s32[1,52]{1,0:T(1,128)S(1)}, s32[1,52]{1,0:T(1,128)S(1)}, u32[]{:S(2)}, u32[]{:S(2)}) collective-permute-start(s32[1,52]{1,0:T(1,128)S(1)} %copy-done), channel_id=1, source_target_pairs={{0,8},{8,16},{16,24},{24,0},{1,9},{9,17},{17,25},{25,1},{2,10},{10... | collective-permute-start | bytes 632 | tf_op jit(solution)/shard_map/ppermute | solution.py:379
  14.1 9.8 %collective-permute-start.4 = (bf16[784,128]{1,0:T(8,128)(2,1)S(1)}, bf16[784,128]{1,0:T(8,128)(2,1)S(1)}, u32[]{:S(2)}, u32[]{:S(2)}) collective-permute-start(bf16[784,128]{1,0:T(8,128)(2,1)S(1)} %get-tuple-element.16), channel_id=1, source_target_pairs={{0,6},{1,7},{2,4},{3,5},{4,2},{5,3},{6,0},{7,1},{8,14},{9,15},{10,... | collective-permute-start | bytes 602120 | tf_op jit(solution)/shard_map/ppermute | solution.py:356
  17.9 10.1 %collective-permute-start.3 = (bf16[784,128]{1,0:T(8,128)(2,1)S(1)}, bf16[784,128]{1,0:T(8,128)(2,1)S(1)}, u32[]{:S(2)}, u32[]{:S(2)}) collective-permute-start(bf16[784,128]{1,0:T(8,128)(2,1)S(1)} %get-tuple-element.17), channel_id=1, source_target_pairs={{0,4},{1,5},{2,6},{3,7},{4,0},{5,1},{6,2},{7,3},{8,12},{9,13},{10,... | collective-permute-start | bytes 602120 | tf_op jit(solution)/shard_map/ppermute | solution.py:356
  18.4 10.2 %collective-permute-start.2 = (bf16[784,128]{1,0:T(8,128)(2,1)S(1)}, bf16[784,128]{1,0:T(8,128)(2,1)S(1)}, u32[]{:S(2)}, u32[]{:S(2)}) collective-permute-start(bf16[784,128]{1,0:T(8,128)(2,1)S(1)} %get-tuple-element.18), channel_id=1, source_target_pairs={{0,2},{1,3},{2,0},{3,1},{4,6},{5,7},{6,4},{7,5},{8,10},{9,11},{10,... | collective-permute-start | bytes 602120 | tf_op jit(solution)/shard_map/ppermute | solution.py:356
  18.6 33.3 %slice-start.2 = ((s8[10485760]{0:T(1024)(128)(4,1)}), s8[2097152]{0:T(1024)(128)(4,1)S(1)}, s32[]{:S(2)}) async-start(s8[10485760]{0:T(1024)(128)(4,1)} %bitcast.12), calls=%async_computation.2 | async-start | bytes 4194304
  18.8 23.2 %collective-permute-start.16 = (bf16[1040,128]{1,0:T(8,128)(2,1)S(1)}, bf16[1040,128]{1,0:T(8,128)(2,1)S(1)}, u32[]{:S(2)}, u32[]{:S(2)}) collective-permute-start(bf16[1040,128]{1,0:T(8,128)(2,1)S(1)} %get-tuple-element.13), channel_id=1, source_target_pairs={{0,6},{1,7},{2,4},{3,5},{4,2},{5,3},{6,0},{7,1},{8,14},{9,15},{10,... | collective-permute-start | bytes 798728 | tf_op jit(solution)/shard_map/ppermute | solution.py:356
  31.7 7.3 %collective-permute-start.5 = (bf16[656,128]{1,0:T(8,128)(2,1)S(1)}, bf16[656,128]{1,0:T(8,128)(2,1)S(1)}, u32[]{:S(2)}, u32[]{:S(2)}) collective-permute-start(bf16[656,128]{1,0:T(8,128)(2,1)S(1)} %shard_map.57), channel_id=1, source_target_pairs={{8,0},{16,8},{24,16},{0,24},{9,1},{17,9},{25,17},{1,25},{10,2},{18... | collective-permute-start | bytes 503816 | tf_op jit(solution)/shard_map/ppermute | solution.py:387
  35.6 11.4 %collective-permute-start.15 = (bf16[1040,128]{1,0:T(8,128)(2,1)S(1)}, bf16[1040,128]{1,0:T(8,128)(2,1)S(1)}, u32[]{:S(2)}, u32[]{:S(2)}) collective-permute-start(bf16[1040,128]{1,0:T(8,128)(2,1)S(1)} %get-tuple-element.14), channel_id=1, source_target_pairs={{0,4},{1,5},{2,6},{3,7},{4,0},{5,1},{6,2},{7,3},{8,12},{9,13},{10,... | collective-permute-start | bytes 798728 | tf_op jit(solution)/shard_map/ppermute | solution.py:356
  37.0 14.9 %collective-permute-start.14 = (bf16[1040,128]{1,0:T(8,128)(2,1)S(1)}, bf16[1040,128]{1,0:T(8,128)(2,1)S(1)}, u32[]{:S(2)}, u32[]{:S(2)}) collective-permute-start(bf16[1040,128]{1,0:T(8,128)(2,1)S(1)} %get-tuple-element.15), channel_id=1, source_target_pairs={{0,2},{1,3},{2,0},{3,1},{4,6},{5,7},{6,4},{7,5},{8,10},{9,11},{10,... | collective-permute-start | bytes 798728 | tf_op jit(solution)/shard_map/ppermute | solution.py:356
  39.1 10.8 %collective-permute-start.8 = (bf16[656,128]{1,0:T(8,128)(2,1)S(1)}, bf16[656,128]{1,0:T(8,128)(2,1)S(1)}, u32[]{:S(2)}, u32[]{:S(2)}) collective-permute-start(bf16[656,128]{1,0:T(8,128)(2,1)S(1)} %collective-permute-done.5.refs_0_), channel_id=1, source_target_pairs={{0,6},{1,7},{2,4},{3,5},{4,2},{5,3},{6,0},{7,1},{8,14},{9,15},{10,... | collective-permute-start | bytes 503816 | tf_op jit(solution)/shard_map/ppermute | solution.py:356
  39.9 10.7 %collective-permute-start.7 = (bf16[656,128]{1,0:T(8,128)(2,1)S(1)}, bf16[656,128]{1,0:T(8,128)(2,1)S(1)}, u32[]{:S(2)}, u32[]{:S(2)}) collective-permute-start(bf16[656,128]{1,0:T(8,128)(2,1)S(1)} %collective-permute-done.5.refs_0_), channel_id=1, source_target_pairs={{0,4},{1,5},{2,6},{3,7},{4,0},{5,1},{6,2},{7,3},{8,12},{9,13},{10,... | collective-permute-start | bytes 503816 | tf_op jit(solution)/shard_map/ppermute | solution.py:356
  42.0 9.8 %collective-permute-start.6 = (bf16[656,128]{1,0:T(8,128)(2,1)S(1)}, bf16[656,128]{1,0:T(8,128)(2,1)S(1)}, u32[]{:S(2)}, u32[]{:S(2)}) collective-permute-start(bf16[656,128]{1,0:T(8,128)(2,1)S(1)} %collective-permute-done.5.refs_0_), channel_id=1, source_target_pairs={{0,2},{1,3},{2,0},{3,1},{4,6},{5,7},{6,4},{7,5},{8,10},{9,11},{10,... | collective-permute-start | bytes 503816 | tf_op jit(solution)/shard_map/ppermute | solution.py:356
  47.0 11.3 %collective-permute-start.9 = (bf16[656,128]{1,0:T(8,128)(2,1)S(1)}, bf16[656,128]{1,0:T(8,128)(2,1)S(1)}, u32[]{:S(2)}, u32[]{:S(2)}) collective-permute-start(bf16[656,128]{1,0:T(8,128)(2,1)S(1)} %collective-permute-done.5.refs_0_), channel_id=1, source_target_pairs={{0,1},{1,0},{2,3},{3,2},{4,5},{5,4},{6,7},{7,6},{8,9},{9,8},{10,11... | collective-permute-start | bytes 503816 | tf_op jit(solution)/shard_map/ppermute | solution.py:356
  49.9 8.4 %collective-permute-start.12 = (bf16[656,128]{1,0:T(8,128)(2,1)S(1)}, bf16[656,128]{1,0:T(8,128)(2,1)S(1)}, u32[]{:S(2)}, u32[]{:S(2)}) collective-permute-start(bf16[656,128]{1,0:T(8,128)(2,1)S(1)} %collective-permute-done.8.refs_3_), channel_id=1, source_target_pairs={{0,1},{1,0},{2,3},{3,2},{4,5},{5,4},{6,7},{7,6},{8,9},{9,8},{10,11... | collective-permute-start | bytes 503816 | tf_op jit(solution)/shard_map/ppermute | solution.py:356
  50.6 7.7 %collective-permute-start.11 = (bf16[656,128]{1,0:T(8,128)(2,1)S(1)}, bf16[656,128]{1,0:T(8,128)(2,1)S(1)}, u32[]{:S(2)}, u32[]{:S(2)}) collective-permute-start(bf16[656,128]{1,0:T(8,128)(2,1)S(1)} %collective-permute-done.7.refs_2_), channel_id=1, source_target_pairs={{0,1},{1,0},{2,3},{3,2},{4,5},{5,4},{6,7},{7,6},{8,9},{9,8},{10,11... | collective-permute-start | bytes 503816 | tf_op jit(solution)/shard_map/ppermute | solution.py:356
  51.8 6.5 %collective-permute-start.10 = (bf16[656,128]{1,0:T(8,128)(2,1)S(1)}, bf16[656,128]{1,0:T(8,128)(2,1)S(1)}, u32[]{:S(2)}, u32[]{:S(2)}) collective-permute-start(bf16[656,128]{1,0:T(8,128)(2,1)S(1)} %collective-permute-done.6.refs_1_), channel_id=1, source_target_pairs={{0,1},{1,0},{2,3},{3,2},{4,5},{5,4},{6,7},{7,6},{8,9},{9,8},{10,11... | collective-permute-start | bytes 503816 | tf_op jit(solution)/shard_map/ppermute | solution.py:356
where the time goes:
time: 63.1 us; the launch traced here: 62.9 us
  Pallas kernels  23.8 us (38%)
  starting transfers between devices  20.4 us (32%)
  waiting for transfers between devices  18.1 us (29%)
    ppermute x15, waiting for transfers between devices, swap(): return lax.ppermute(value, 'dp', [(i, i ^ distance) for i in range(count)])  16.6 us
    ppermute x15, starting transfers between devices, swap(): return lax.ppermute(value, 'dp', [(i, i ^ distance) for i in range(count)])  13.6 us
    pallas_call x3, Pallas kernels, partial_factors(): pl.pallas_call(functools.partial(factor_kernel, blocks, dp_count, paritie...  9.83 us
    pallas_call x1, Pallas kernels, half_update(): pl.pallas_call(functools.partial(half_kernel, slots, token_total), out_sh...  6.43 us
    pallas_call x1, Pallas kernels, final_update(): pl.pallas_call(functools.partial(update_kernel, blocks, dp_count), out_sh...  4.43 us
    ppermute x1, starting transfers between devices, whole(): unit = lax.ppermute(unit, 'section', back)  3.84 us
    pallas_call x1, Pallas kernels, invert_units(): pl.pallas_call(functools.partial(invert_kernel, hidden_blocks, blocks, dp...  3.1 us
    ppermute x1, starting transfers between devices, whole(): their_sweeps = lax.ppermute(sweeps, 'section', ahead)  3 us
  transfers between devices with their start and end apart: 17, of which 9 were waited for; matrix products, arithmetic and copies ran while one was open for 1% of the time, Pallas kernels for 15%

commit v1 on v0

v1 whole, which is shorter than its diff:
```python
import functools

import jax
import jax.numpy as jnp
from jax import lax
from jax.experimental import pallas as pl
from jax.experimental.pallas import tpu as pltpu
from jax.sharding import PartitionSpec as P


BLOCK = 256
HALF = BLOCK // 2
PAD = 16
NS_MAX = 4

damping = 0.05


def masks():
    row = lax.broadcasted_iota(jnp.int32, (HALF, HALF), 0)
    col = lax.broadcasted_iota(jnp.int32, (HALF, HALF), 1)
    return row, col


def pack_block(full, row, col):
    upper = full[:HALF, HALF:]
    second = full[HALF:, HALF:]
    mixed = jnp.where(row >= col, full[:HALF, :HALF], second)
    line = jnp.sum(jnp.where(row == col, second, 0.0), axis=0, keepdims=True)
    return upper, mixed, line


def unpack_block(upper, mixed, line, row, col):
    turned = mixed.T
    first = jnp.where(row >= col, mixed, turned)
    second = jnp.where(row < col, mixed, jnp.where(row > col, turned, line))
    top = jnp.concatenate([first, upper], axis=1)
    bottom = jnp.concatenate([upper.T, second], axis=1)
    return jnp.concatenate([top, bottom], axis=0)


def store_unit(out, index, blocks, row, col):
    count = len(blocks)
    lines = jnp.zeros((PAD, HALF), jnp.float32)
    place = lax.broadcasted_iota(jnp.int32, (PAD, HALF), 0)
    for j, full in enumerate(blocks):
        upper, mixed, line = pack_block(full, row, col)
        out[index + (pl.ds(j * BLOCK, HALF),)] = upper.astype(out.dtype)
        out[index + (pl.ds(j * BLOCK + HALF, HALF),)] = mixed.astype(out.dtype)
        lines = jnp.where(place == j, line, lines)
    out[index + (pl.ds(count * BLOCK, PAD),)] = lines.astype(out.dtype)


def gram(x):
    return lax.dot_general(x, x, (((0,), (0,)), ((), ())), preferred_element_type=jnp.float32)


def shares(blocks, dp_count):
    share, rest = blocks // dp_count, blocks % dp_count
    return share, -(-rest // (dp_count // 2))


def owned_block(owner, slot, blocks, dp_count):
    share, _ = shares(blocks, dp_count)
    if slot < share:
        return owner * share + slot
    chips = dp_count // 2
    return jnp.minimum(share * dp_count + owner // 2 + chips * (slot - share), blocks - 1)


def store_factors(columns, out, parity, blocks, dp_count, row, col):
    me = lax.axis_index("dp")
    for step in range(dp_count // 2):
        grams = []
        for slot in range(sum(shares(blocks, dp_count))):
            block = owned_block(me ^ (2 * step + parity), slot, blocks, dp_count)
            place = pl.ds(pl.multiple_of(block * BLOCK, BLOCK), BLOCK)
            grams.append(sum(gram(part[:, place]) for part in columns))
        store_unit(out, (step,), grams, row, col)


def send_kernel(blocks, dp_count, here, head, sent, grads, sems):
    chunks = sems.shape[0]
    rows = grads.shape[0] // chunks

    def fetch(source, i):
        place = pl.ds(i * rows, rows)
        view = source.at[0, place] if len(source.shape) == 3 else source.at[place]
        return pltpu.make_async_copy(view, grads.at[place], sems.at[i])

    def fetch_all(source):
        for i in range(chunks):
            fetch(source, i).start()

    first = lax.axis_index("section") == 0
    pl.when(first)(lambda: fetch_all(head))
    pl.when(jnp.logical_not(first))(lambda: fetch_all(here))
    for i in range(chunks):
        fetch(here, i).wait()
    store_factors([grads], sent, 1, blocks, dp_count, *masks())


def keep_kernel(blocks, dp_count, grads, acts, kept, early, sem):
    ahead = pltpu.make_async_copy(acts.at[0, pl.ds(0, early.shape[0])], early, sem)
    ahead.start()
    store_factors([grads], kept, 0, blocks, dp_count, *masks())
    ahead.wait()


def late_kernel(blocks, dp_count, early, acts, sent, late, sem):
    rows = late.shape[0]
    copy = pltpu.make_async_copy(acts.at[0, pl.ds(acts.shape[1] - rows, rows)], late, sem)
    copy.start()
    copy.wait()
    store_factors([early, late], sent, 1, blocks, dp_count, *masks())


def last_kernel(blocks, dp_count, early, late, kept):
    store_factors([early, late], kept, 0, blocks, dp_count, *masks())


def packed_shape(blocks, dp_count):
    unit = sum(shares(blocks, dp_count)) * BLOCK + PAD
    return pltpu.VMEM((dp_count // 2, unit, HALF), jnp.bfloat16)


def factor_call(kernel, operands, spaces, outs, scratch, rows, width, part):
    return pl.pallas_call(
        kernel,
        out_shape=outs,
        in_specs=[pl.BlockSpec(memory_space=space) for space in spaces],
        out_specs=tuple(pl.BlockSpec(memory_space=pltpu.VMEM) for _ in outs),
        scratch_shapes=scratch,
        compiler_params=pltpu.CompilerParams(vmem_limit_bytes=16 << 20),
        cost_estimate=pl.CostEstimate(
            flops=int(2 * part * rows * width * BLOCK), bytes_accessed=rows * width * 3, transcendentals=0
        ),
    )(
        *[
            pltpu.with_memory_space_constraint(operand, space)
            for operand, space in zip(operands, spaces)
        ]
    )


def model_factors(input_grads, head_grads, acts, dp_count):
    rows, width = head_grads.shape
    blocks = width // BLOCK
    early = rows // 3 // PAD * PAD
    hbm, vmem = pltpu.HBM, pltpu.VMEM
    packed = packed_shape(blocks, dp_count)
    sent, grads = factor_call(
        functools.partial(send_kernel, blocks, dp_count),
        [input_grads, head_grads],
        [hbm] * 2,
        (packed, pltpu.VMEM((rows, width), jnp.bfloat16)),
        [pltpu.SemaphoreType.DMA((4,))],
        rows,
        width,
        0.5,
    )
    kept, first = factor_call(
        functools.partial(keep_kernel, blocks, dp_count),
        [grads, acts],
        [vmem, hbm],
        (packed, pltpu.VMEM((early, acts.shape[2]), jnp.bfloat16)),
        [pltpu.SemaphoreType.DMA],
        rows,
        width,
        0.5,
    )
    return sent, kept, first


def hidden_factors(early, acts, dp_count):
    _, rows, width = acts.shape
    blocks = width // BLOCK
    packed = packed_shape(blocks, dp_count)
    vmem = pltpu.VMEM
    sent, late = factor_call(
        functools.partial(late_kernel, blocks, dp_count),
        [early, acts],
        [vmem, pltpu.HBM],
        (packed, pltpu.VMEM((rows - early.shape[0], width), jnp.bfloat16)),
        [pltpu.SemaphoreType.DMA],
        rows,
        width,
        0.5,
    )
    (kept,) = factor_call(
        functools.partial(last_kernel, blocks, dp_count),
        [early, late],
        [vmem] * 2,
        (packed,),
        [],
        rows,
        width,
        0.5,
    )
    return sent, kept


def product(a, b):
    return jnp.dot(
        a.astype(jnp.bfloat16), b.astype(jnp.bfloat16), preferred_element_type=jnp.float32
    )


def newton(matrices, counts):
    row = lax.broadcasted_iota(jnp.int32, (BLOCK, BLOCK), 0)
    col = lax.broadcasted_iota(jnp.int32, (BLOCK, BLOCK), 1)
    diagonal = row == col
    levels, rest, heights, found = [], [], [], []
    for matrix in matrices:
        size = jnp.sum(jnp.abs(matrix), axis=0, keepdims=True)
        scale = 1.0 / jnp.max(size, axis=1, keepdims=True)
        line = jnp.sum(jnp.where(diagonal, matrix, 0.0), axis=0, keepdims=True)
        shift = scale * jnp.sum(line, axis=1, keepdims=True) * (1.0 / BLOCK)
        left = jnp.where(diagonal, shift, 0.0) - scale * matrix
        levels.append(1.0 - shift)
        rest.append(left)
        heights.append(scale * (2.0 - shift))
        found.append(scale * left)
    for turn in range(1, NS_MAX):
        rest = [2.0 * a * left + product(left, left) for a, left in zip(levels, rest)]
        levels = [a * a for a in levels]
        step = [
            x * left + a * part + product(part, left)
            for a, left, x, part in zip(levels, rest, heights, found)
        ]
        more = [turn < count for count in counts]
        found = [jnp.where(go, part + add, part) for go, part, add in zip(more, found, step)]
        heights = [jnp.where(go, x + a * x, x) for go, x, a in zip(more, heights, levels)]
    return [part + jnp.where(diagonal, x, 0.0) for x, part in zip(heights, found)]


def summed_factors(refs, slots, token_total, row, col):
    terms = [ref[0] if len(ref.shape) == 3 else ref[...] for ref in refs]
    total = sum(term.astype(jnp.float32) for term in terms) * (1.0 / token_total)
    wide_row = lax.broadcasted_iota(jnp.int32, (BLOCK, BLOCK), 0)
    wide_col = lax.broadcasted_iota(jnp.int32, (BLOCK, BLOCK), 1)
    shift = jnp.where(wide_row == wide_col, damping, 0.0)
    blocks = []
    for j in range(slots):
        upper = total[j * BLOCK : j * BLOCK + HALF]
        mixed = total[j * BLOCK + HALF : (j + 1) * BLOCK]
        line = total[slots * BLOCK + j : slots * BLOCK + j + 1]
        blocks.append(unpack_block(upper, mixed, line, row, col) + shift)
    return blocks


def gather_rows(blocks, dp_count):
    share, extra = shares(blocks, dp_count)
    return share * BLOCK + extra * HALF + PAD


def invert_kernel(hidden_blocks, blocks, dp_count, token_total, sweeps, *refs):
    out = refs[-1]
    row, col = masks()
    share, extra = shares(blocks, dp_count)
    slots = share + extra
    me = lax.axis_index("dp")
    factors = summed_factors(refs[:-1], slots, token_total, row, col)
    counts = [
        sweeps[0, hidden_blocks + owned_block(me, j, blocks, dp_count)] for j in range(slots)
    ]
    lines = jnp.zeros((PAD, HALF), jnp.float32)
    place = lax.broadcasted_iota(jnp.int32, (PAD, HALF), 0)
    even = me % 2 == 0
    for j, full in enumerate(newton(factors, counts)):
        upper, mixed, line = pack_block(full, row, col)
        lines = jnp.where(place == j, line, lines)
        if j < share:
            out[pl.ds(j * BLOCK, HALF)] = upper.astype(out.dtype)
            out[pl.ds(j * BLOCK + HALF, HALF)] = mixed.astype(out.dtype)
        else:
            own = jnp.where(even, upper, mixed)
            out[pl.ds(share * BLOCK + (j - share) * HALF, HALF)] = own.astype(out.dtype)
    out[pl.ds(share * BLOCK + extra * HALF, PAD)] = lines.astype(out.dtype)


def in_vmem(arrays):
    return [pltpu.with_memory_space_constraint(array, pltpu.VMEM) for array in arrays]


def invert_units(sweeps, arrays, hidden_blocks, blocks, dp_count, token_total):
    unit = gather_rows(blocks, dp_count)
    slots = sum(shares(blocks, dp_count))
    return pl.pallas_call(
        functools.partial(invert_kernel, hidden_blocks, blocks, dp_count, token_total),
        out_shape=pltpu.VMEM((unit, HALF), jnp.bfloat16),
        grid_spec=pltpu.PrefetchScalarGridSpec(
            num_scalar_prefetch=1,
            grid=(1,),
            in_specs=[pl.BlockSpec(memory_space=pltpu.VMEM)] * len(arrays),
            out_specs=pl.BlockSpec(memory_space=pltpu.VMEM),
        ),
        compiler_params=pltpu.CompilerParams(vmem_limit_bytes=16 << 20),
        cost_estimate=pl.CostEstimate(
            flops=12 * slots * BLOCK**3, bytes_accessed=12 * slots * BLOCK * BLOCK, transcendentals=0
        ),
    )(sweeps, *in_vmem(arrays))


def load_kernel(source, out, sem):
    copy = pltpu.make_async_copy(source.at[0, pl.ds(0, out.shape[0])], out, sem)
    copy.start()
    copy.wait()


def load_rows(source, rows):
    width = source.shape[2]
    return pl.pallas_call(
        load_kernel,
        out_shape=pltpu.VMEM((rows, width), source.dtype),
        in_specs=[pl.BlockSpec(memory_space=pltpu.HBM)],
        out_specs=pl.BlockSpec(memory_space=pltpu.VMEM),
        scratch_shapes=[pltpu.SemaphoreType.DMA],
        compiler_params=pltpu.CompilerParams(vmem_limit_bytes=16 << 20),
        cost_estimate=pl.CostEstimate(flops=0, bytes_accessed=2 * rows * width, transcendentals=0),
    )(pltpu.with_memory_space_constraint(source, pltpu.HBM))


def half_kernel(slots, token_total, sweeps, *refs):
    early, weights, out, late, sem = refs[-5:]
    rows = late.shape[0]
    start = early.shape[0]
    copy = pltpu.make_async_copy(weights.at[0, pl.ds(start, rows)], late, sem)
    copy.start()
    row, col = masks()
    me = lax.axis_index("dp")
    factors = summed_factors(refs[:-5], slots, token_total, row, col)
    found = newton(factors, [sweeps[0, me * slots + j] for j in range(slots)])
    found = [full.astype(jnp.bfloat16) for full in found]
    for part, place in ((early, pl.ds(0, start)), (late, pl.ds(start, rows))):
        if part is late:
            copy.wait()
        for j in range(slots):
            columns = slice(j * BLOCK, (j + 1) * BLOCK)
            value = jnp.dot(part[:, columns], found[j], preferred_element_type=jnp.float32)
            out[place, columns] = value.astype(jnp.bfloat16)


def half_update(sweeps, arrays, token_total, early, weight_grad):
    _, depth, columns = weight_grad.shape
    slots = columns // BLOCK
    specs = [pl.BlockSpec(memory_space=pltpu.VMEM)] * (len(arrays) + 1)
    specs.append(pl.BlockSpec(memory_space=pltpu.HBM))
    return pl.pallas_call(
        functools.partial(half_kernel, slots, token_total),
        out_shape=pltpu.VMEM((depth, columns), jnp.bfloat16),
        grid_spec=pltpu.PrefetchScalarGridSpec(
            num_scalar_prefetch=1,
            grid=(1,),
            in_specs=specs,
            out_specs=pl.BlockSpec(memory_space=pltpu.VMEM),
            scratch_shapes=[
                pltpu.VMEM((depth - early.shape[0], columns), jnp.bfloat16),
                pltpu.SemaphoreType.DMA,
            ],
        ),
        compiler_params=pltpu.CompilerParams(vmem_limit_bytes=24 << 20),
        cost_estimate=pl.CostEstimate(
            flops=12 * slots * BLOCK**3 + 2 * depth * columns * BLOCK,
            bytes_accessed=2 * depth * columns,
            transcendentals=0,
        ),
    )(
        sweeps,
        *in_vmem(arrays),
        pltpu.with_memory_space_constraint(early, pltpu.VMEM),
        pltpu.with_memory_space_constraint(weight_grad, pltpu.HBM),
    )


def update_kernel(blocks, dp_count, cores, turns, places, *refs):
    half, out, staged, sems = refs[-4:]
    units = dict(zip([r + core for core in cores for r in turns], refs))
    share, extra = shares(blocks, dp_count)
    me = lax.axis_index("dp")
    row, col = masks()
    even = me % 2 == 0

    def copy(step, block):
        place = pl.ds(pl.multiple_of(block * BLOCK, BLOCK), BLOCK)
        return pltpu.make_async_copy(staged.at[step], out.at[0, place], sems.at[step])

    def tile(unit, start, rows=HALF):
        return unit[start : start + rows, :].astype(jnp.float32)

    def one(step, r, slot):
        near, far = units.get(r), units.get(r + 1)
        owner = me ^ r
        if slot >= 2 * share:
            slot -= share
            start = share * BLOCK + (slot - share) * HALF
            own, other = tile(near, start), tile(far, start)
            upper, mixed = jnp.where(even, own, other), jnp.where(even, other, own)
        else:
            if slot >= share:
                near, owner, slot = far, owner ^ 1, slot - share
            upper, mixed = tile(near, slot * BLOCK), tile(near, slot * BLOCK + HALF)
        block = owned_block(owner, slot, blocks, dp_count)
        line = tile(near, share * BLOCK + extra * HALF, PAD)[slot : slot + 1]
        full = unpack_block(upper, mixed, line, row, col).astype(jnp.bfloat16)
        place = pl.ds(pl.multiple_of(block * BLOCK, BLOCK), BLOCK)
        value = jnp.dot(full, half[place, :], preferred_element_type=jnp.float32)
        staged[step] = value.astype(jnp.bfloat16)
        copy(step, block).start()

    def guarded(r, slot, run):
        chips, rest = dp_count // 2, blocks % dp_count
        if slot < 2 * share or rest == chips * extra:
            run()
        else:
            pl.when((me ^ r) // 2 + chips * (slot - 2 * share) < rest)(run)

    steps = [(r, slot) for r in turns for slot in places]
    for step, (r, slot) in enumerate(steps):
        guarded(r, slot, functools.partial(one, step, r, slot))
    for step, (r, slot) in enumerate(steps):
        guarded(r, slot, lambda: copy(step, 0).wait())


def update_rows(even, odd, half, dp_count, turns, places, done=None):
    depth, columns = half.shape
    blocks = depth // BLOCK
    steps = len(turns) * len(places)
    units = [*even, *odd]
    operands = units + ([] if done is None else [done])
    specs = [pl.BlockSpec(memory_space=pltpu.VMEM)] * len(units)
    specs += [pl.BlockSpec(memory_space=pl.ANY)] * (len(operands) - len(specs))
    cores = (0, 1) if odd else (0,)
    return pl.pallas_call(
        functools.partial(update_kernel, blocks, dp_count, cores, turns, places),
        out_shape=jax.ShapeDtypeStruct((1, depth, columns), jnp.bfloat16),
        in_specs=specs + [pl.BlockSpec(memory_space=pltpu.VMEM)],
        out_specs=pl.BlockSpec(memory_space=pl.ANY),
        scratch_shapes=[
            pltpu.VMEM((steps, BLOCK, columns), jnp.bfloat16),
            pltpu.SemaphoreType.DMA((steps,)),
        ],
        input_output_aliases={} if done is None else {len(units): 0},
        compiler_params=pltpu.CompilerParams(vmem_limit_bytes=24 << 20),
        cost_estimate=pl.CostEstimate(
            flops=2 * steps * BLOCK * BLOCK * columns,
            bytes_accessed=2 * steps * BLOCK * columns,
            transcendentals=0,
        ),
    )(*operands, pltpu.with_memory_space_constraint(half, pltpu.VMEM))


def swap(value, distance):
    count = lax.axis_size("dp")
    return lax.ppermute(value, "dp", [(i, i ^ distance) for i in range(count)])


def spread(keep, first, dp_count):
    others = []
    for r in range(2, dp_count, 2):
        value = keep[r // 2].astype(jnp.float32) + first[r // 2].astype(jnp.float32)
        others.append(swap(value.astype(jnp.bfloat16), r))
    return others


def whole(acts, input_grads, head_grads, weight_grad, sweeps):
    dp_count = lax.axis_size("dp")
    section_count = lax.axis_size("section")
    tokens = acts.shape[1] * dp_count
    hidden_blocks = acts.shape[2] // BLOCK
    model_blocks = input_grads.shape[2] // BLOCK
    back = [((s + 1) % section_count, s) for s in range(section_count)]
    ahead = [(s, (s + 1) % section_count) for s in range(section_count)]

    send_g, keep_g, early = model_factors(input_grads, head_grads, acts, dp_count)
    first_g = swap(send_g, 1)
    their_sweeps = lax.ppermute(sweeps, "section", ahead)
    send_a, keep_a = hidden_factors(early, acts, dp_count)
    others_g = spread(keep_g, first_g, dp_count)
    first_a = swap(send_a, 1)
    unit = invert_units(
        their_sweeps,
        [keep_g, first_g, *others_g],
        hidden_blocks,
        model_blocks,
        dp_count,
        tokens,
    )
    others_a = spread(keep_a, first_a, dp_count)
    unit = lax.ppermute(unit, "section", back)
    weights = load_rows(weight_grad, weight_grad.shape[1] // 5 * 3)
    even = [unit] + [swap(unit, r) for r in range(2, dp_count, 2)]
    half = half_update(sweeps, [keep_a, first_a, *others_a], tokens, weights, weight_grad)
    odd = [swap(unit, 1)]
    odd += [swap(value, 1) for value in even[1:]]
    share, extra = shares(model_blocks, dp_count)
    turns, places = list(range(0, dp_count, 2)), list(range(2 * share + extra))
    return update_rows(even, odd, half, dp_count, turns, places)


def solution(mesh):
    return jax.shard_map(
        whole,
        mesh=mesh,
        in_specs=(
            P("section", "dp", None),
            P("section", "dp", None),
            P("dp", None),
            P("section", None, "dp"),
            P("section", None),
        ),
        out_specs=P("section", None, "dp"),
        check_vma=False,
    )
```

time: 63.1 us -> 60.8 us (0.964)
  waiting for transfers between devices: 18.1 us -> 15.3 us
  Pallas kernels: 23.8 us -> 25.7 us
  starting transfers between devices: 20.4 us -> 19 us
    ppermute x15, waiting for transfers between devices: 16.6 us -> 10 us  [swap(): return lax.ppermute(value, 'dp', [(i, i ^ distance) for i in range(count)])]
    ppermute x1, waiting for transfers between devices: 0.01 us -> 3.79 us  [whole(): their_sweeps = lax.ppermute(sweeps, 'section', ahead)]
    pallas_call x4 -> x6, Pallas kernels: 14.3 us -> 17.3 us  [the longest x4 10.1 us: factor_call(): pl.pallas_call(kernel, out_shape=outs, in_specs=[pl.BlockSpec(memory_spac...]
    ppermute x1, starting transfers between devices: 3 us -> 1.57 us  [whole(): their_sweeps = lax.ppermute(sweeps, 'section', ahead)]
    pallas_call x1, Pallas kernels: 3.1 us -> 2.34 us  [invert_units(): pl.pallas_call(functools.partial(invert_kernel, hidden_blocks, blocks, dp...]
  transfers between devices with their start and end apart: 17 -> 17, of which waited for: 9 -> 9; matrix products, arithmetic and copies ran while one was open for 1% -> 1% of each run, Pallas kernels for 15% -> 21%
where the time goes in v1:
time: 60.8 us; the launch traced here: 60.6 us
  Pallas kernels  25.7 us (42%)
  starting transfers between devices  19 us (31%)
  waiting for transfers between devices  15.3 us (25%)
    ppermute x15, starting transfers between devices, swap(): return lax.ppermute(value, 'dp', [(i, i ^ distance) for i in range(count)])  13.5 us
    pallas_call x4, Pallas kernels, factor_call(): pl.pallas_call(kernel, out_shape=outs, in_specs=[pl.BlockSpec(memory_spac...  10.1 us
    ppermute x15, waiting for transfers between devices, swap(): return lax.ppermute(value, 'dp', [(i, i ^ distance) for i in range(count)])  10 us
    pallas_call x1, Pallas kernels, half_update(): pl.pallas_call(functools.partial(half_kernel, slots, token_total), out_sh...  6.04 us
    pallas_call x1, Pallas kernels, update_rows(): pl.pallas_call(functools.partial(update_kernel, blocks, dp_count, cores,...  4.43 us
    ppermute x1, starting transfers between devices, whole(): unit = lax.ppermute(unit, 'section', back)  3.85 us
    ppermute x1, waiting for transfers between devices, whole(): their_sweeps = lax.ppermute(sweeps, 'section', ahead)  3.79 us
    pallas_call x1, Pallas kernels, load_rows(): pl.pallas_call(load_kernel, out_shape=pltpu.VMEM((rows, width), source.dt...  2.79 us
  transfers between devices with their start and end apart: 17, of which 9 were waited for; matrix products, arithmetic and copies ran while one was open for 1% of the time, Pallas kernels for 21%

profile of v1, /device:TPU:0, one launch (start us, length us, event | category | flops | bytes accessed | tf_op | source)
XLA Modules:
  0.0 60.6 jit_solution(5388241227316690426)
XLA Ops:
  0.0 3.2 %shard_map.55 = (bf16[4,784,128]{2,1,0:T(8,128)(2,1)S(1)}, bf16[384,5120]{1,0:T(8,128)(2,1)S(1)}) custom-call(bf16[1,384,5120]{2,1,0:T(8,128)(2,1)} %here.1, bf16[384,5120]{1,0:T(8,128)(2,1)} %head.1), custom_call_target="tpu_custom_call" | custom-call | flops 503316480 | bytes 5898240 | tf_op jit(solution)/shard_map/pallas_call | solution.py:128
  3.2 2.0 %shard_map.56 = (bf16[4,784,128]{2,1,0:T(8,128)(2,1)S(1)}, bf16[128,8192]{1,0:T(8,128)(2,1)S(1)}) custom-call(bf16[384,5120]{1,0:T(8,128)(2,1)S(1)} %get-tuple-element.11.grads, bf16[1,384,8192]{2,1,0:T(8,128)(2,1)} %acts.3), custom_call_target="tpu_custom_call" | custom-call | flops 503316480 | bytes 5898240 | tf_op jit(solution)/shard_map/pallas_call | solution.py:128
  5.2 3.6 %shard_map.58 = (bf16[4,1040,128]{2,1,0:T(8,128)(2,1)S(1)}, bf16[256,8192]{1,0:T(8,128)(2,1)S(1)}) custom-call(bf16[128,8192]{1,0:T(8,128)(2,1)S(1)} %get-tuple-element.14.early, bf16[1,384,8192]{2,1,0:T(8,128)(2,1)} %acts.3), custom_call_target="tpu_custom_call" | custom-call | flops 805306368 | bytes 9437184 | tf_op jit(solution)/shard_map/pallas_call | solution.py:128
  9.4 1.3 %shard_map.59.refs_0_ = bf16[4,1040,128]{2,1,0:T(8,128)(2,1)S(1)} custom-call(bf16[128,8192]{1,0:T(8,128)(2,1)S(1)} %get-tuple-element.14.early, bf16[256,8192]{1,0:T(8,128)(2,1)S(1)} %get-tuple-element.15.late), custom_call_target="tpu_custom_call" | custom-call | flops 805306368 | bytes 9437184 | tf_op jit(solution)/shard_map/pallas_call | solution.py:128
  10.7 2.0 %collective-permute-done.1.refs_1_ = bf16[4,784,128]{2,1,0:T(8,128)(2,1)S(1)} collective-permute-done((bf16[4,784,128]{2,1,0:T(8,128)(2,1)S(1)}, bf16[4,784,128]{2,1,0:T(8,128)(2,1)S(1)}, u32[]{:S(2)}, u32[]{:S(2)}) %collective-permute-start.1) | collective-permute-done | bytes 802848 | tf_op jit(solution)/shard_map/ppermute | solution.py:455
  12.9 3.9 %collective-permute-start.4 = (bf16[784,128]{1,0:T(8,128)(2,1)S(1)}, bf16[784,128]{1,0:T(8,128)(2,1)S(1)}, u32[]{:S(2)}, u32[]{:S(2)}) collective-permute-start(bf16[784,128]{1,0:T(8,128)(2,1)S(1)} %get-tuple-element.20), channel_id=1, source_target_pairs={{0,6},{1,7},{2,4},{3,5},{4,2},{5,3},{6,0},{7,1},{8,14},{9,15},{10,... | collective-permute-start | bytes 602120 | tf_op jit(solution)/shard_map/ppermute | solution.py:455
  17.6 2.9 %collective-permute-start.16 = (bf16[1040,128]{1,0:T(8,128)(2,1)S(1)}, bf16[1040,128]{1,0:T(8,128)(2,1)S(1)}, u32[]{:S(2)}, u32[]{:S(2)}) collective-permute-start(bf16[1040,128]{1,0:T(8,128)(2,1)S(1)} %get-tuple-element.17), channel_id=1, source_target_pairs={{0,6},{1,7},{2,4},{3,5},{4,2},{5,3},{6,0},{7,1},{8,14},{9,15},{10,... | collective-permute-start | bytes 798728 | tf_op jit(solution)/shard_map/ppermute | solution.py:455
  20.5 1.6 %collective-permute-start = (s32[1,52]{1,0:T(1,128)S(1)}, s32[1,52]{1,0:T(1,128)S(1)}, u32[]{:S(2)}, u32[]{:S(2)}) collective-permute-start(s32[1,52]{1,0:T(1,128)S(1)} %copy-done), channel_id=1, source_target_pairs={{0,8},{8,16},{16,24},{24,0},{1,9},{9,17},{17,25},{25,1},{2,10},{10... | collective-permute-start | bytes 632 | tf_op jit(solution)/shard_map/ppermute | solution.py:477
  22.1 3.8 %collective-permute-done.sweeps = s32[1,52]{1,0:T(1,128)S(1)} collective-permute-done((s32[1,52]{1,0:T(1,128)S(1)}, s32[1,52]{1,0:T(1,128)S(1)}, u32[]{:S(2)}, u32[]{:S(2)}) %collective-permute-start) | collective-permute-done | bytes 240 | tf_op jit(solution)/shard_map/ppermute | solution.py:477
  25.9 1.0 %collective-permute-done.3.refs_3_ = bf16[784,128]{1,0:T(8,128)(2,1)S(1)} collective-permute-done((bf16[784,128]{1,0:T(8,128)(2,1)S(1)}, bf16[784,128]{1,0:T(8,128)(2,1)S(1)}, u32[]{:S(2)}, u32[]{:S(2)}) %collective-permute-start.3) | collective-permute-done | bytes 200736 | tf_op jit(solution)/shard_map/ppermute | solution.py:455
  26.9 0.6 %collective-permute-done.2.refs_2_ = bf16[784,128]{1,0:T(8,128)(2,1)S(1)} collective-permute-done((bf16[784,128]{1,0:T(8,128)(2,1)S(1)}, bf16[784,128]{1,0:T(8,128)(2,1)S(1)}, u32[]{:S(2)}, u32[]{:S(2)}) %collective-permute-start.2) | collective-permute-done | bytes 200736 | tf_op jit(solution)/shard_map/ppermute | solution.py:455
  27.5 2.3 %shard_map.57 = bf16[656,128]{1,0:T(8,128)(2,1)S(1)} custom-call(s32[1,52]{1,0:T(1,128)S(1)} %collective-permute-done.sweeps, bf16[4,784,128]{2,1,0:T(8,128)(2,1)S(1)} %get-tuple-element.12.refs_0_, bf16[4,784,128]{2,1,0:T(8,128)(2,1)S(1)} %collective-permute-done.1.refs_1_, bf16[784,128]{1,0:T(8,128)(2,1)S(1)} %collective-permute-done.2.refs_2_, ...), custom_call_target="tpu_custom_call" | custom-call | flops 603979776 | bytes 2359296 | tf_op jit(solution)/shard_map/pallas_call | solution.py:289
  29.8 3.8 %collective-permute-start.5 = (bf16[656,128]{1,0:T(8,128)(2,1)S(1)}, bf16[656,128]{1,0:T(8,128)(2,1)S(1)}, u32[]{:S(2)}, u32[]{:S(2)}) collective-permute-start(bf16[656,128]{1,0:T(8,128)(2,1)S(1)} %shard_map.57), channel_id=1, source_target_pairs={{8,0},{16,8},{24,16},{0,24},{9,1},{17,9},{25,17},{1,25},{10,2},{18... | collective-permute-start | bytes 503816 | tf_op jit(solution)/shard_map/ppermute | solution.py:490
  33.7 1.4 %collective-permute-start.15 = (bf16[1040,128]{1,0:T(8,128)(2,1)S(1)}, bf16[1040,128]{1,0:T(8,128)(2,1)S(1)}, u32[]{:S(2)}, u32[]{:S(2)}) collective-permute-start(bf16[1040,128]{1,0:T(8,128)(2,1)S(1)} %get-tuple-element.18), channel_id=1, source_target_pairs={{0,4},{1,5},{2,6},{3,7},{4,0},{5,1},{6,2},{7,3},{8,12},{9,13},{10,... | collective-permute-start | bytes 798728 | tf_op jit(solution)/shard_map/ppermute | solution.py:455
  35.7 1.5 %collective-permute-done.5.refs_0_ = bf16[656,128]{1,0:T(8,128)(2,1)S(1)} collective-permute-done((bf16[656,128]{1,0:T(8,128)(2,1)S(1)}, bf16[656,128]{1,0:T(8,128)(2,1)S(1)}, u32[]{:S(2)}, u32[]{:S(2)}) %collective-permute-start.5) | collective-permute-done | bytes 167968 | tf_op jit(solution)/shard_map/ppermute | solution.py:490
  37.2 0.8 %collective-permute-start.8 = (bf16[656,128]{1,0:T(8,128)(2,1)S(1)}, bf16[656,128]{1,0:T(8,128)(2,1)S(1)}, u32[]{:S(2)}, u32[]{:S(2)}) collective-permute-start(bf16[656,128]{1,0:T(8,128)(2,1)S(1)} %collective-permute-done.5.refs_0_), channel_id=1, source_target_pairs={{0,6},{1,7},{2,4},{3,5},{4,2},{5,3},{6,0},{7,1},{8,14},{9,15},{10,... | collective-permute-start | bytes 503816 | tf_op jit(solution)/shard_map/ppermute | solution.py:455
  38.0 2.1 %collective-permute-start.7 = (bf16[656,128]{1,0:T(8,128)(2,1)S(1)}, bf16[656,128]{1,0:T(8,128)(2,1)S(1)}, u32[]{:S(2)}, u32[]{:S(2)}) collective-permute-start(bf16[656,128]{1,0:T(8,128)(2,1)S(1)} %collective-permute-done.5.refs_0_), channel_id=1, source_target_pairs={{0,4},{1,5},{2,6},{3,7},{4,0},{5,1},{6,2},{7,3},{8,12},{9,13},{10,... | collective-permute-start | bytes 503816 | tf_op jit(solution)/shard_map/ppermute | solution.py:455
  40.6 2.8 %shard_map.60.refs_5_ = bf16[3072,1024]{1,0:T(8,128)(2,1)S(1)} custom-call(bf16[1,5120,1024]{2,1,0:T(8,128)(2,1)} %refs_6_.1), custom_call_target="tpu_custom_call" | custom-call | bytes 6291456 | tf_op jit(solution)/shard_map/pallas_call | solution.py:313
  43.4 1.6 %collective-permute-done.15.refs_3_ = bf16[1040,128]{1,0:T(8,128)(2,1)S(1)} collective-permute-done((bf16[1040,128]{1,0:T(8,128)(2,1)S(1)}, bf16[1040,128]{1,0:T(8,128)(2,1)S(1)}, u32[]{:S(2)}, u32[]{:S(2)}) %collective-permute-start.15) | collective-permute-done | bytes 266272 | tf_op jit(solution)/shard_map/ppermute | solution.py:455
  45.1 2.9 %collective-permute-done.8.refs_3_ = bf16[656,128]{1,0:T(8,128)(2,1)S(1)} collective-permute-done((bf16[656,128]{1,0:T(8,128)(2,1)S(1)}, bf16[656,128]{1,0:T(8,128)(2,1)S(1)}, u32[]{:S(2)}, u32[]{:S(2)}) %collective-permute-start.8) | collective-permute-done | bytes 167968 | tf_op jit(solution)/shard_map/ppermute | solution.py:455
  48.0 0.6 %collective-permute-done.7.refs_2_ = bf16[656,128]{1,0:T(8,128)(2,1)S(1)} collective-permute-done((bf16[656,128]{1,0:T(8,128)(2,1)S(1)}, bf16[656,128]{1,0:T(8,128)(2,1)S(1)}, u32[]{:S(2)}, u32[]{:S(2)}) %collective-permute-start.7) | collective-permute-done | bytes 167968 | tf_op jit(solution)/shard_map/ppermute | solution.py:455
  48.7 1.2 %collective-permute-done.6.refs_1_ = bf16[656,128]{1,0:T(8,128)(2,1)S(1)} collective-permute-done((bf16[656,128]{1,0:T(8,128)(2,1)S(1)}, bf16[656,128]{1,0:T(8,128)(2,1)S(1)}, u32[]{:S(2)}, u32[]{:S(2)}) %collective-permute-start.6) | collective-permute-done | bytes 167968 | tf_op jit(solution)/shard_map/ppermute | solution.py:455
  49.9 6.0 %shard_map.61.refs_8_ = bf16[5120,1024]{1,0:T(8,128)(2,1)S(1)} custom-call(s32[1,52]{1,0:T(1,128)S(1)} %copy-done, bf16[4,1040,128]{2,1,0:T(8,128)(2,1)S(1)} %shard_map.59.refs_0_, bf16[4,1040,128]{2,1,0:T(8,128)(2,1)S(1)} %collective-permute-done.13.refs_1_, bf16[1040,128]{1,0:T(8,128)(2,1)S(1)} %collective-permute-done.14.refs_2_, ...), custom_call_target="tpu_custom_call" | custom-call | flops 3489660928 | bytes 10485760 | tf_op jit(solution)/shard_map/pallas_call | solution.py:349
  56.0 4.4 %shard_map.62 = bf16[1,5120,1024]{2,1,0:T(8,128)(2,1)} custom-call(bf16[656,128]{1,0:T(8,128)(2,1)S(1)} %collective-permute-done.5.refs_0_, bf16[656,128]{1,0:T(8,128)(2,1)S(1)} %collective-permute-done.6.refs_1_, bf16[656,128]{1,0:T(8,128)(2,1)S(1)} %collective-permute-done.7.refs_2_, bf16[656,128]{1,0:T(8,128)(2,1)S(1)} %collective-permute-done.8.refs_3_, ...), custom_call_target="tpu_custom_call" | custom-call | flops 2684354560 | bytes 10485760 | tf_op jit(solution)/shard_map/pallas_call | solution.py:434
  (22 shorter events, 2.8 us)
Async XLA Ops:
  8.7 8.7 %collective-permute-start.13 = (bf16[4,1040,128]{2,1,0:T(8,128)(2,1)S(1)}, bf16[4,1040,128]{2,1,0:T(8,128)(2,1)S(1)}, u32[]{:S(2)}, u32[]{:S(2)}) collective-permute-start(bf16[4,1040,128]{2,1,0:T(8,128)(2,1)S(1)} %get-tuple-element.16), channel_id=1, source_target_pairs={{0,1},{1,0},{2,3},{3,2},{4,5},{5,4},{6,7},{7,6},{8,9},{9,8},{10,11... | collective-permute-start | bytes 3194888 | tf_op jit(solution)/shard_map/ppermute | solution.py:455
  9.3 3.5 %collective-permute-start.1 = (bf16[4,784,128]{2,1,0:T(8,128)(2,1)S(1)}, bf16[4,784,128]{2,1,0:T(8,128)(2,1)S(1)}, u32[]{:S(2)}, u32[]{:S(2)}) collective-permute-start(bf16[4,784,128]{2,1,0:T(8,128)(2,1)S(1)} %get-tuple-element.13), channel_id=1, source_target_pairs={{0,1},{1,0},{2,3},{3,2},{4,5},{5,4},{6,7},{7,6},{8,9},{9,8},{10,11... | collective-permute-start | bytes 2408456 | tf_op jit(solution)/shard_map/ppermute | solution.py:455
  10.7 9.8 %copy-start = (s32[1,52]{1,0:T(1,128)S(1)}, s32[1,52]{1,0:T(1,128)}, u32[]{:S(2)}) copy-start(s32[1,52]{1,0:T(1,128)} %sweeps.1) | copy-start | bytes 628
  12.9 13.0 %collective-permute-start.4 = (bf16[784,128]{1,0:T(8,128)(2,1)S(1)}, bf16[784,128]{1,0:T(8,128)(2,1)S(1)}, u32[]{:S(2)}, u32[]{:S(2)}) collective-permute-start(bf16[784,128]{1,0:T(8,128)(2,1)S(1)} %get-tuple-element.20), channel_id=1, source_target_pairs={{0,6},{1,7},{2,4},{3,5},{4,2},{5,3},{6,0},{7,1},{8,14},{9,15},{10,... | collective-permute-start | bytes 602120 | tf_op jit(solution)/shard_map/ppermute | solution.py:455
  16.8 10.1 %collective-permute-start.3 = (bf16[784,128]{1,0:T(8,128)(2,1)S(1)}, bf16[784,128]{1,0:T(8,128)(2,1)S(1)}, u32[]{:S(2)}, u32[]{:S(2)}) collective-permute-start(bf16[784,128]{1,0:T(8,128)(2,1)S(1)} %get-tuple-element.21), channel_id=1, source_target_pairs={{0,4},{1,5},{2,6},{3,7},{4,0},{5,1},{6,2},{7,3},{8,12},{9,13},{10,... | collective-permute-start | bytes 602120 | tf_op jit(solution)/shard_map/ppermute | solution.py:455
  17.3 10.2 %collective-permute-start.2 = (bf16[784,128]{1,0:T(8,128)(2,1)S(1)}, bf16[784,128]{1,0:T(8,128)(2,1)S(1)}, u32[]{:S(2)}, u32[]{:S(2)}) collective-permute-start(bf16[784,128]{1,0:T(8,128)(2,1)S(1)} %get-tuple-element.22), channel_id=1, source_target_pairs={{0,2},{1,3},{2,0},{3,1},{4,6},{5,7},{6,4},{7,5},{8,10},{9,11},{10,... | collective-permute-start | bytes 602120 | tf_op jit(solution)/shard_map/ppermute | solution.py:455
  17.6 22.5 %collective-permute-start.16 = (bf16[1040,128]{1,0:T(8,128)(2,1)S(1)}, bf16[1040,128]{1,0:T(8,128)(2,1)S(1)}, u32[]{:S(2)}, u32[]{:S(2)}) collective-permute-start(bf16[1040,128]{1,0:T(8,128)(2,1)S(1)} %get-tuple-element.17), channel_id=1, source_target_pairs={{0,6},{1,7},{2,4},{3,5},{4,2},{5,3},{6,0},{7,1},{8,14},{9,15},{10,... | collective-permute-start | bytes 798728 | tf_op jit(solution)/shard_map/ppermute | solution.py:455
  20.5 5.4 %collective-permute-start = (s32[1,52]{1,0:T(1,128)S(1)}, s32[1,52]{1,0:T(1,128)S(1)}, u32[]{:S(2)}, u32[]{:S(2)}) collective-permute-start(s32[1,52]{1,0:T(1,128)S(1)} %copy-done), channel_id=1, source_target_pairs={{0,8},{8,16},{16,24},{24,0},{1,9},{9,17},{17,25},{25,1},{2,10},{10... | collective-permute-start | bytes 632 | tf_op jit(solution)/shard_map/ppermute | solution.py:477
  29.8 7.3 %collective-permute-start.5 = (bf16[656,128]{1,0:T(8,128)(2,1)S(1)}, bf16[656,128]{1,0:T(8,128)(2,1)S(1)}, u32[]{:S(2)}, u32[]{:S(2)}) collective-permute-start(bf16[656,128]{1,0:T(8,128)(2,1)S(1)} %shard_map.57), channel_id=1, source_target_pairs={{8,0},{16,8},{24,16},{0,24},{9,1},{17,9},{25,17},{1,25},{10,2},{18... | collective-permute-start | bytes 503816 | tf_op jit(solution)/shard_map/ppermute | solution.py:490
  33.7 11.4 %collective-permute-start.15 = (bf16[1040,128]{1,0:T(8,128)(2,1)S(1)}, bf16[1040,128]{1,0:T(8,128)(2,1)S(1)}, u32[]{:S(2)}, u32[]{:S(2)}) collective-permute-start(bf16[1040,128]{1,0:T(8,128)(2,1)S(1)} %get-tuple-element.18), channel_id=1, source_target_pairs={{0,4},{1,5},{2,6},{3,7},{4,0},{5,1},{6,2},{7,3},{8,12},{9,13},{10,... | collective-permute-start | bytes 798728 | tf_op jit(solution)/shard_map/ppermute | solution.py:455
  35.1 14.9 %collective-permute-start.14 = (bf16[1040,128]{1,0:T(8,128)(2,1)S(1)}, bf16[1040,128]{1,0:T(8,128)(2,1)S(1)}, u32[]{:S(2)}, u32[]{:S(2)}) collective-permute-start(bf16[1040,128]{1,0:T(8,128)(2,1)S(1)} %get-tuple-element.19), channel_id=1, source_target_pairs={{0,2},{1,3},{2,0},{3,1},{4,6},{5,7},{6,4},{7,5},{8,10},{9,11},{10,... | collective-permute-start | bytes 798728 | tf_op jit(solution)/shard_map/ppermute | solution.py:455
  37.2 10.9 %collective-permute-start.8 = (bf16[656,128]{1,0:T(8,128)(2,1)S(1)}, bf16[656,128]{1,0:T(8,128)(2,1)S(1)}, u32[]{:S(2)}, u32[]{:S(2)}) collective-permute-start(bf16[656,128]{1,0:T(8,128)(2,1)S(1)} %collective-permute-done.5.refs_0_), channel_id=1, source_target_pairs={{0,6},{1,7},{2,4},{3,5},{4,2},{5,3},{6,0},{7,1},{8,14},{9,15},{10,... | collective-permute-start | bytes 503816 | tf_op jit(solution)/shard_map/ppermute | solution.py:455
  38.0 10.7 %collective-permute-start.7 = (bf16[656,128]{1,0:T(8,128)(2,1)S(1)}, bf16[656,128]{1,0:T(8,128)(2,1)S(1)}, u32[]{:S(2)}, u32[]{:S(2)}) collective-permute-start(bf16[656,128]{1,0:T(8,128)(2,1)S(1)} %collective-permute-done.5.refs_0_), channel_id=1, source_target_pairs={{0,4},{1,5},{2,6},{3,7},{4,0},{5,1},{6,2},{7,3},{8,12},{9,13},{10,... | collective-permute-start | bytes 503816 | tf_op jit(solution)/shard_map/ppermute | solution.py:455
  40.1 9.8 %collective-permute-start.6 = (bf16[656,128]{1,0:T(8,128)(2,1)S(1)}, bf16[656,128]{1,0:T(8,128)(2,1)S(1)}, u32[]{:S(2)}, u32[]{:S(2)}) collective-permute-start(bf16[656,128]{1,0:T(8,128)(2,1)S(1)} %collective-permute-done.5.refs_0_), channel_id=1, source_target_pairs={{0,2},{1,3},{2,0},{3,1},{4,6},{5,7},{6,4},{7,5},{8,10},{9,11},{10,... | collective-permute-start | bytes 503816 | tf_op jit(solution)/shard_map/ppermute | solution.py:455
  45.1 10.9 %collective-permute-start.9 = (bf16[656,128]{1,0:T(8,128)(2,1)S(1)}, bf16[656,128]{1,0:T(8,128)(2,1)S(1)}, u32[]{:S(2)}, u32[]{:S(2)}) collective-permute-start(bf16[656,128]{1,0:T(8,128)(2,1)S(1)} %collective-permute-done.5.refs_0_), channel_id=1, source_target_pairs={{0,1},{1,0},{2,3},{3,2},{4,5},{5,4},{6,7},{7,6},{8,9},{9,8},{10,11... | collective-permute-start | bytes 503816 | tf_op jit(solution)/shard_map/ppermute | solution.py:455
  48.0 8.0 %collective-permute-start.12 = (bf16[656,128]{1,0:T(8,128)(2,1)S(1)}, bf16[656,128]{1,0:T(8,128)(2,1)S(1)}, u32[]{:S(2)}, u32[]{:S(2)}) collective-permute-start(bf16[656,128]{1,0:T(8,128)(2,1)S(1)} %collective-permute-done.8.refs_3_), channel_id=1, source_target_pairs={{0,1},{1,0},{2,3},{3,2},{4,5},{5,4},{6,7},{7,6},{8,9},{9,8},{10,11... | collective-permute-start | bytes 503816 | tf_op jit(solution)/shard_map/ppermute | solution.py:455
  48.7 7.3 %collective-permute-start.11 = (bf16[656,128]{1,0:T(8,128)(2,1)S(1)}, bf16[656,128]{1,0:T(8,128)(2,1)S(1)}, u32[]{:S(2)}, u32[]{:S(2)}) collective-permute-start(bf16[656,128]{1,0:T(8,128)(2,1)S(1)} %collective-permute-done.7.refs_2_), channel_id=1, source_target_pairs={{0,1},{1,0},{2,3},{3,2},{4,5},{5,4},{6,7},{7,6},{8,9},{9,8},{10,11... | collective-permute-start | bytes 503816 | tf_op jit(solution)/shard_map/ppermute | solution.py:455
  49.9 6.1 %collective-permute-start.10 = (bf16[656,128]{1,0:T(8,128)(2,1)S(1)}, bf16[656,128]{1,0:T(8,128)(2,1)S(1)}, u32[]{:S(2)}, u32[]{:S(2)}) collective-permute-start(bf16[656,128]{1,0:T(8,128)(2,1)S(1)} %collective-permute-done.6.refs_1_), channel_id=1, source_target_pairs={{0,1},{1,0},{2,3},{3,2},{4,5},{5,4},{6,7},{7,6},{8,9},{9,8},{10,11... | collective-permute-start | bytes 503816 | tf_op jit(solution)/shard_map/ppermute | solution.py:455
